TPU v7x, 128 devices: a whole 4x4x4 slice. The times are simulated.
128 devices in a mesh: seq: 16 (over x, z), hx: 8 (over y, core).
Axes of the slice: x: 4, y: 4, z: 4, core: 2. Of those that a mesh axis runs over, the one named last changes fastest.
Arguments:
- query: bfloat16 [16384, 8192], P('seq', 'hx'), may hold values from -6 to 6
- key_in: bfloat16 [16384, 8192], P('seq', 'hx'), may hold values from -6 to 6
- value: bfloat16 [16384, 8192], P('seq', 'hx'), may hold values from -6 to 6
- head_gain: float32 [8192], P('hx'), may hold values from 0.1 to 1.9
- out_weight: bfloat16 [8192, 6144], P('hx', 'seq'), may hold values from -0.0625 to 0.0625
- residual: bfloat16 [16384, 6144], P(('seq', 'hx')), may hold values from -6 to 6
Outputs:
- mixed: bfloat16 [16384, 6144], P(('seq', 'hx'))
All inputs are finite; a program needn't handle non-finite values.
Results may differ from a plain program's by a relative error of at most 0.014.
Values may be sent and summed in bfloat16 or wider, within the bound.
No kernel may reach another device: no remote copies, remote signals or barrier semaphores. Data moves between devices by JAX's collectives and lax.ppermute only.
A program may use at most 128 MiB of HBM per device.

v0:
```python
import jax
import jax.numpy as jnp
from jax import lax
from jax.sharding import PartitionSpec as P

DH = 128


def activate(array):
    return jax.nn.silu(array.astype(jnp.float32)).astype(jnp.bfloat16)


def per_device(query, key_in, value, head_gain, out_weight, residual):
    highest = lax.Precision.HIGHEST
    tokens_here, width = query.shape
    heads = width // DH
    q_act = activate(query).reshape(tokens_here, heads, DH)
    k_act = activate(key_in).reshape(tokens_here, heads, DH)
    v_heads = value.reshape(tokens_here, heads, DH)
    blocks = min(512, tokens_here)
    count = tokens_here // blocks
    rows = jnp.arange(blocks, dtype=jnp.int32)
    lower = rows[:, None] >= rows[None, :]
    running = jnp.zeros((heads, DH, DH), jnp.float32)
    pieces = []
    for index in range(count):
        q_part = q_act[index * blocks : (index + 1) * blocks]
        k_part = k_act[index * blocks : (index + 1) * blocks]
        v_part = v_heads[index * blocks : (index + 1) * blocks]
        scores = jnp.einsum("thd,shd->hts", q_part, k_part, preferred_element_type=jnp.float32)
        scores = jnp.where(lower[None, :, :], scores, jnp.zeros_like(scores))
        inner = jnp.einsum("hts,she->the", scores, v_part.astype(jnp.float32), precision=highest)
        if index > 0:
            inner = inner + jnp.einsum(
                "thd,hde->the", q_part.astype(jnp.float32), running, precision=highest
            )
        pieces.append(inner)
        running = running + jnp.einsum(
            "thd,the->hde", k_part, v_part, preferred_element_type=jnp.float32
        )
    local_part = jnp.concatenate(pieces, axis=0)
    empty = jnp.zeros((heads, DH, DH), jnp.float32)
    position = lax.axis_index("seq")
    piece = lax.all_gather(running[None].astype(jnp.bfloat16), "seq", axis=0, tiled=True).astype(
        jnp.float32
    )
    ranks = jnp.arange(piece.shape[0], dtype=jnp.int32)
    keep = (ranks < position)[:, None, None, None]
    prefix = empty + jnp.sum(jnp.where(keep, piece, jnp.zeros_like(piece)), axis=0)
    attended = local_part + jnp.einsum(
        "thd,hde->the", q_act.astype(jnp.float32), prefix, precision=highest
    )
    meansq = jnp.mean(attended * attended, axis=-1, keepdims=True)
    normed = attended * lax.rsqrt(meansq + 1e-06) * head_gain.reshape(heads, DH)
    normed = normed.astype(jnp.bfloat16).reshape(tokens_here, width)
    full_weight = lax.all_gather(out_weight, "seq", axis=1, tiled=True)
    summed = lax.psum_scatter(
        jnp.dot(normed, full_weight, preferred_element_type=jnp.float32).astype(jnp.bfloat16),
        "hx",
        scatter_dimension=0,
        tiled=True,
    ).astype(jnp.float32)
    return (summed + residual.astype(jnp.float32)).astype(jnp.bfloat16)


def solution(mesh):
    return jax.shard_map(
        per_device,
        mesh=mesh,
        in_specs=(
            P("seq", "hx"),
            P("seq", "hx"),
            P("seq", "hx"),
            P("hx"),
            P("hx", "seq"),
            P(("seq", "hx"), None),
        ),
        out_specs=P(("seq", "hx"), None),
        check_vma=False,
    )
```

profile of v0, /device:TPU:1, one launch (start us, length us, event | category | flops | bytes accessed | tf_op | source)
XLA Modules:
  0.0 277.5 jit_solution(6667149055458355304)
XLA Ops:
  6.5 2.9 %copy.46 = bf16[1024,1024]{0,1:T(8,128)(2,1)S(1)} copy(bf16[1024,1024]{1,0:T(8,128)(2,1)} %param.7) | data formatting | bytes 4194304 | tf_op args[1]
  9.4 1.2 fusion.12
  10.6 1.1 fusion.25
  11.8 1.3 fusion.24
  13.1 0.5 copy.79
  13.6 1.9 copy.78
  15.5 0.4 fusion.28
  16.0 0.8 copy-done.7
  16.8 2.4 fusion.20
  19.2 0.0 all-gather.6.cloned.1.call-update
  19.2 0.0 all-gather.4.cloned.1.call-start
  19.2 0.7 all-gather.4.cloned.1.call-update
  19.9 0.0 reduce-scatter.2.cloned.1.call-start
  20.0 4.0 %copy.45 = bf16[1024,1024]{0,1:T(8,128)(2,1)} copy(bf16[1024,1024]{1,0:T(8,128)(2,1)} %param.6) | data formatting | bytes 4194304 | tf_op args[0]
  24.0 0.1 iota_compare_fusion
  24.1 2.9 %fusion.8 = bf16[1024,1024]{0,1:T(8,128)(2,1)S(1)} fusion(bf16[1024,1024]{0,1:T(8,128)(2,1)} %copy.45), kind=kLoop, calls=%fused_computation.14 | loop fusion | flops 6291456 | bytes 4194304 | tf_op jit(solution)/shard_map/convert_element_type | solution.py:10
  27.0 0.1 fusion.23
  27.1 1.3 fusion.27
  28.4 4.5 %fusion.1 = f32[8,512,128]{2,1,0:T(8,128)S(1)} fusion(bf16[512,8,128]{0,2,1:T(8,128)(2,1)S(1)} %bitcast.41, f32[8,512,512]{2,1,0:T(8,128)S(1)} %fusion.27, pred[512,512]{1,0:T(8,128)(4,1)S(1)} %iota_compare_fusion), kind=kOutput, calls=%fused_computation.3 | convolution fusion | flops 3223322624 | bytes 11796480 | tf_op jit(solution)/shard_map/hts,she->the/dot_general | solution.py:32
  33.0 2.5 bitcast_add_fusion
  35.5 1.3 fusion.26
  36.8 6.0 %fusion.17 = f32[512,8,128]{2,0,1:T(8,128)} fusion(bf16[512,8,128]{0,2,1:T(8,128)(2,1)S(1)} %bitcast.37, f32[8,512,512]{2,1,0:T(8,128)S(1)} %fusion.26, pred[512,512]{1,0:T(8,128)(4,1)S(1)} %iota_compare_fusion), kind=kOutput, calls=%fused_computation.28 | convolution fusion | flops 3223322624 | bytes 11796480 | tf_op jit(solution)/shard_map/hts,she->the/dot_general | solution.py:32
  42.8 31.4 %all-gather.6.cloned.1.call-done = bf16[128,128,128]{2,1,0:T(8,128)(2,1)} async-done(((bf16[8,128,128]{2,1,0:T(8,128)(2,1)}), bf16[128,128,128]{2,1,0:T(8,128)(2,1)}) %all-gather.6.cloned.1.call-update) | async-done | bytes 4194320 | tf_op jit(solution)/shard_map/all_gather | solution.py:44
  74.2 3.3 %fusion = f32[8,128,128]{2,1,0:T(8,128)S(1)} fusion(bf16[16,8,128,128]{3,2,1,0:T(8,128)(2,1)} %bitcast.46, pred[16]{0:T(512)(128)(4,1)S(1)} %iota_compare_fusion.1), kind=kLoop, calls=%fused_computation.2 | loop fusion | flops 6160384 | bytes 4718608 | tf_op jit(solution)/shard_map/reduce_sum | solution.py:49
  77.6 0.1 copy-done.6
  77.7 3.3 %multiply_reduce_fusion = (f32[1024,8]{0,1:T(8,128)S(1)}, f32[1024,8,128]{2,0,1:T(8,128)S(1)}) fusion(f32[8,128,128]{2,1,0:T(8,128)S(1)} %fusion, bf16[1024,8,128]{0,2,1:T(8,128)(2,1)S(1)} %bitcast.35, f32[512,8,128]{2,0,1:T(8,128)S(1)} %copy-done.5, f32[512,8,128]{2,0,1:T(8,128)S(1)} %copy-done.6), kind=kOutput, calls=%fused_computation.21 | convolution fusion | flops 1614798848 | bytes 11042816 | tf_op jit(solution)/shard_map/thd,hde->the/dot_general | solution.py:50
  81.0 1.4 multiply_convert_fusion
  82.4 2.7 copy.63
  85.2 89.7 %all-gather.4.cloned.1.call-done = bf16[1024,6144]{1,0:T(8,128)(2,1)} async-done(((bf16[1024,384]{1,0:T(8,128)(2,1)}), bf16[1024,6144]{1,0:T(8,128)(2,1)}) %all-gather.4.cloned.1.call-update) | async-done | bytes 12582928 | tf_op jit(solution)/shard_map/all_gather | solution.py:56
  174.9 21.1 %convolution_convert_fusion = bf16[1024,6144]{1,0:T(8,128)(2,1)} fusion(bf16[1024,1024]{0,1:T(8,128)(2,1)} %bitcast.48, bf16[1024,6144]{1,0:T(8,128)(2,1)} %all-gather.4.cloned.1.call-done), kind=kOutput, calls=%fused_computation | convolution fusion | flops 12891193344 | bytes 27262976 | tf_op jit(solution)/shard_map/dot_general | solution.py:58
  195.9 72.1 %reduce-scatter.2.cloned.1.call-done = bf16[128,6144]{1,0:T(8,128)(2,1)} async-done(((bf16[1024,6144]{1,0:T(8,128)(2,1)}), bf16[128,6144]{1,0:T(8,128)(2,1)}) %reduce-scatter.2.cloned.1.call-update) | async-done | bytes 1572880 | tf_op jit(solution)/shard_map/reduce_scatter | solution.py:57
  268.0 2.9 %add_convert_fusion = bf16[128,6144]{1,0:T(8,128)(2,1)} fusion(bf16[128,6144]{1,0:T(8,128)(2,1)S(1)} %copy-done.10, bf16[128,6144]{1,0:T(8,128)(2,1)} %reduce-scatter.2.cloned.1.call-done), kind=kLoop, calls=%fused_computation.26 | loop fusion | flops 3145728 | bytes 4718592 | tf_op jit(solution)/shard_map/convert_element_type | solution.py:63
  (26 shorter events, 0.1 us)
Async XLA Ops:
  6.5 67.7 %all-gather.6.cloned.1.call-start = ((), (), s32[]{:S(2)}) async-start(), calls=%async_computation.3 | async-start | bytes 4456448 | tf_op jit(solution)/shard_map/all_gather | solution.py:44
  9.4 2.4 copy-start.9
  11.8 3.8 %copy-start = (bf16[512,1024]{0,1:T(8,128)(2,1)}, bf16[512,1024]{0,1:T(8,128)(2,1)S(1)}, u32[]{:S(2)}) copy-start(bf16[512,1024]{0,1:T(8,128)(2,1)S(1)} %get-tuple-element.9) | copy-start | bytes 3145732
  13.6 6.3 %copy-start.2 = (bf16[512,1024]{0,1:T(8,128)(2,1)}, bf16[512,1024]{0,1:T(8,128)(2,1)S(1)}, u32[]{:S(2)}) copy-start(bf16[512,1024]{0,1:T(8,128)(2,1)S(1)} %copy.79) | copy-start | bytes 3145732
  16.0 0.8 copy-start.7
  19.2 155.7 %all-gather.4.cloned.1.call-start = ((), (), s32[]{:S(2)}) async-start(), calls=%async_computation.1 | async-start | bytes 13369344 | tf_op jit(solution)/shard_map/all_gather | solution.py:56
  19.9 248.1 %reduce-scatter.2.cloned.1.call-start = ((), (), s32[]{:S(2)}) async-start(), calls=%async_computation.2 | async-start | bytes 14155776 | tf_op jit(solution)/shard_map/reduce_scatter | solution.py:57
  24.0 3.1 %copy-start.4 = (bf16[512,1024]{0,1:T(8,128)(2,1)S(1)}, bf16[512,1024]{0,1:T(8,128)(2,1)}, u32[]{:S(2)}) copy-start(bf16[512,1024]{0,1:T(8,128)(2,1)} %get-tuple-element.10) | copy-start | bytes 3145732
  27.1 1.3 copy-start.3
  28.4 4.6 %copy-start.8 = (f32[8,128,128]{2,1,0:T(8,128)S(1)}, f32[8,128,128]{2,1,0:T(8,128)}, u32[]{:S(2)}) copy-start(f32[8,128,128]{2,1,0:T(8,128)} %copy-done.7) | copy-start | bytes 1572868
  33.0 2.5 copy-start.1
  74.2 3.4 %copy-start.5 = (f32[512,8,128]{2,0,1:T(8,128)S(1)}, f32[512,8,128]{2,0,1:T(8,128)}, u32[]{:S(2)}) copy-start(f32[512,8,128]{2,0,1:T(8,128)} %bitcast_add_fusion) | copy-start | bytes 6291460
  74.2 3.5 %copy-start.6 = (f32[512,8,128]{2,0,1:T(8,128)S(1)}, f32[512,8,128]{2,0,1:T(8,128)}, u32[]{:S(2)}) copy-start(f32[512,8,128]{2,0,1:T(8,128)} %fusion.17) | copy-start | bytes 6291460
  77.7 3.3 %copy-start.11 = (f32[1024]{0:T(1024)S(1)}, f32[1024]{0:T(1024)}, u32[]{:S(2)}) copy-start(f32[1024]{0:T(1024)} %param.9) | copy-start | bytes 12292
  195.9 72.1 %copy-start.10 = (bf16[128,6144]{1,0:T(8,128)(2,1)S(1)}, bf16[128,6144]{1,0:T(8,128)(2,1)}, u32[]{:S(2)}) copy-start(bf16[128,6144]{1,0:T(8,128)(2,1)} %param.11) | copy-start | bytes 4718596
Sparse Core Ops, SparseCore 0:
  19.3 54.8 all-gather.5
  76.3 98.4 all-gather.3
  196.1 71.9 reduce-scatter.1
where the time goes:
time: 278 us; the launch traced here: 277 us
  waiting for transfers between devices  194 us (70%)
  matrix products  42.7 us (15%)
  local copies, waits for them, and re-layouts  15.5 us (6%)
  between operations  13.3 us (5%)
  other arithmetic  11.9 us (4%)
    all_gather x1, waiting for transfers between devices, per_device(): full_weight = lax.all_gather(out_weight, 'seq', axis=1, tiled=True)  89.7 us
    reduce_scatter x1, waiting for transfers between devices, per_device(): lax.psum_scatter(jnp.dot(normed, full_weight, preferred_element_type=jnp....  72.1 us
    all_gather x1, waiting for transfers between devices, per_device(): lax.all_gather(running[None].astype(jnp.bfloat16), 'seq', axis=0, tiled=T...  31.4 us
    dot_general x1, matrix products, per_device(): jnp.dot(normed, full_weight, preferred_element_type=jnp.float32)  21.1 us
    dot_general x2, matrix products, per_device(): jnp.einsum('hts,she->the', scores, v_part.astype(jnp.float32), precision=...  10.5 us
    unnamed x28, local copies, waits for them, and re-layouts  10.2 us
  transfers between devices with their start and end apart: 3, of which 3 were waited for; matrix products, arithmetic and copies ran while one was open for 12% of the time, Pallas kernels for 0%

commit v1 on v0

--- a/solution.py
+++ b/solution.py
@@ -4,6 +4,19 @@
 from jax.sharding import PartitionSpec as P
 
 DH = 128
+
+
+def gather_around(x, axis, dim):
+    ways = lax.axis_size(axis)
+    up = [(d, (d + 1) % ways) for d in range(ways)]
+    down = [(d, (d - 1) % ways) for d in range(ways)]
+    earlier, later = ([x], [x])
+    for _ in range(ways // 2):
+        earlier.append(lax.ppermute(earlier[-1], axis, up))
+    for _ in range((ways - 1) // 2):
+        later.append(lax.ppermute(later[-1], axis, down))
+    line = jnp.concatenate([*earlier[::-1], *later[1:]], axis=dim)
+    return jnp.roll(line, (lax.axis_index(axis) - ways // 2) * x.shape[dim], axis=dim)
 
 
 def activate(array):
@@ -53,7 +66,7 @@
     meansq = jnp.mean(attended * attended, axis=-1, keepdims=True)
     normed = attended * lax.rsqrt(meansq + 1e-06) * head_gain.reshape(heads, DH)
     normed = normed.astype(jnp.bfloat16).reshape(tokens_here, width)
-    full_weight = lax.all_gather(out_weight, "seq", axis=1, tiled=True)
+    full_weight = gather_around(out_weight, "seq", 1)
     summed = lax.psum_scatter(
         jnp.dot(normed, full_weight, preferred_element_type=jnp.float32).astype(jnp.bfloat16),
         "hx",

time: 278 us -> 362 us (1.30)
  local copies, waits for them, and re-layouts: 15.5 us -> 74.7 us
  starting transfers between devices: 0.08 us -> 37.6 us
  waiting for transfers between devices: 194 us -> 169 us
  matrix products: 42.7 us -> 52.2 us
    ppermute x0 -> x15, waiting for transfers between devices: none -> 98.2 us  [the longest x8 68.2 us: gather_around(): earlier.append(lax.ppermute(earlier[-1], axis, up))]
    all_gather x1 -> x0, waiting for transfers between devices: 89.7 us -> none  [per_device(): full_weight = lax.all_gather(out_weight, 'seq', axis=1, tiled=True)]
    unnamed x28 -> x69, local copies, waits for them, and re-layouts: 10.2 us -> 67.5 us
    ppermute x0 -> x15, starting transfers between devices: none -> 37.6 us  [the longest x7 35.1 us: gather_around(): later.append(lax.ppermute(later[-1], axis, down))]
    all_gather x1, waiting for transfers between devices: 31.4 us -> 0.01 us  [per_device(): lax.all_gather(running[None].astype(jnp.bfloat16), 'seq', axis=0, tiled=T...]
    dot_general x2, matrix products: 2.58 us -> 8.61 us  [per_device(): jnp.einsum('thd,shd->hts', q_part, k_part, preferred_element_type=jnp.flo...]
  transfers between devices with their start and end apart: 3 -> 17, of which waited for: 3 -> 11; matrix products, arithmetic and copies ran while one was open for 12% -> 29% of each run, Pallas kernels for 0% -> 0%
where the time goes in v1:
time: 362 us; the launch traced here: 361 us
  waiting for transfers between devices  169 us (47%)
  local copies, waits for them, and re-layouts  74.7 us (21%)
  matrix products  52.2 us (14%)
  starting transfers between devices  37.6 us (10%)
  between operations  13.7 us (4%)
  other arithmetic  13.1 us (4%)
    reduce_scatter x1, waiting for transfers between devices, per_device(): lax.psum_scatter(jnp.dot(normed, full_weight, preferred_element_type=jnp....  71.1 us
    ppermute x8, waiting for transfers between devices, gather_around(): earlier.append(lax.ppermute(earlier[-1], axis, up))  68.2 us
    unnamed x69, local copies, waits for them, and re-layouts  67.5 us
    ppermute x7, starting transfers between devices, gather_around(): later.append(lax.ppermute(later[-1], axis, down))  35.1 us
    ppermute x7, waiting for transfers between devices, gather_around(): later.append(lax.ppermute(later[-1], axis, down))  29.9 us
    dot_general x1, matrix products, per_device(): jnp.dot(normed, full_weight, preferred_element_type=jnp.float32)  21.9 us
    dot_general x2, matrix products, per_device(): jnp.einsum('hts,she->the', scores, v_part.astype(jnp.float32), precision=...  12.8 us
    dot_general x2, matrix products, per_device(): jnp.einsum('thd,shd->hts', q_part, k_part, preferred_element_type=jnp.flo...  8.61 us
  transfers between devices with their start and end apart: 17, of which 11 were waited for; matrix products, arithmetic and copies ran while one was open for 29% of the time, Pallas kernels for 0%

profile of v1, /device:TPU:1, one launch (start us, length us, event | category | flops | bytes accessed | tf_op | source)
XLA Modules:
  0.0 360.6 jit_solution(535126083509305440)
XLA Ops:
  6.5 2.5 collective-permute-start
  9.0 21.8 %collective-permute-done = bf16[1024,384]{1,0:T(8,128)(2,1)S(1)} collective-permute-done((bf16[1024,384]{1,0:T(8,128)(2,1)}, bf16[1024,384]{1,0:T(8,128)(2,1)S(1)}, u32[]{:S(2)}, u32[]{:S(2)}) %collective-permute-start) | collective-permute-done | bytes 786464 | tf_op jit(solution)/shard_map/ppermute | solution.py:15
  30.8 4.8 %collective-permute-start.8 = (bf16[1024,384]{1,0:T(8,128)(2,1)}, bf16[1024,384]{1,0:T(8,128)(2,1)}, u32[]{:S(2)}, u32[]{:S(2)}) collective-permute-start(bf16[1024,384]{1,0:T(8,128)(2,1)} %param.10), channel_id=1, source_target_pairs={{0,120},{8,0},{16,8},{24,16},{32,24},{40,32},{48,40},{56,48},{64,5... | collective-permute-start | bytes 2359304 | tf_op jit(solution)/shard_map/ppermute | solution.py:17
  35.6 16.3 %collective-permute-done.1 = bf16[1024,384]{1,0:T(8,128)(2,1)S(1)} collective-permute-done((bf16[1024,384]{1,0:T(8,128)(2,1)S(1)}, bf16[1024,384]{1,0:T(8,128)(2,1)S(1)}, u32[]{:S(2)}, u32[]{:S(2)}) %collective-permute-start.1) | collective-permute-done | bytes 786464 | tf_op jit(solution)/shard_map/ppermute | solution.py:15
  51.9 3.1 copy.46
  55.1 2.6 fusion.17
  57.7 4.5 %collective-permute-start.9 = (bf16[1024,384]{1,0:T(8,128)(2,1)}, bf16[1024,384]{1,0:T(8,128)(2,1)}, u32[]{:S(2)}, u32[]{:S(2)}) collective-permute-start(bf16[1024,384]{1,0:T(8,128)(2,1)} %collective-permute-done.8), channel_id=1, source_target_pairs={{0,120},{8,0},{16,8},{24,16},{32,24},{40,32},{48,40},{56,48},{64,5... | collective-permute-start | bytes 2359304 | tf_op jit(solution)/shard_map/ppermute | solution.py:17
  62.2 10.1 %collective-permute-done.2 = bf16[1024,384]{1,0:T(8,128)(2,1)} collective-permute-done((bf16[1024,384]{1,0:T(8,128)(2,1)S(1)}, bf16[1024,384]{1,0:T(8,128)(2,1)}, u32[]{:S(2)}, u32[]{:S(2)}) %collective-permute-start.2) | collective-permute-done | bytes 786464 | tf_op jit(solution)/shard_map/ppermute | solution.py:15
  77.2 5.2 %collective-permute-start.10 = (bf16[1024,384]{1,0:T(8,128)(2,1)}, bf16[1024,384]{1,0:T(8,128)(2,1)}, u32[]{:S(2)}, u32[]{:S(2)}) collective-permute-start(bf16[1024,384]{1,0:T(8,128)(2,1)} %collective-permute-done.9), channel_id=1, source_target_pairs={{0,120},{8,0},{16,8},{24,16},{32,24},{40,32},{48,40},{56,48},{64,5... | collective-permute-start | bytes 2359304 | tf_op jit(solution)/shard_map/ppermute | solution.py:17
  82.4 9.4 %collective-permute-done.3 = bf16[1024,384]{1,0:T(8,128)(2,1)} collective-permute-done((bf16[1024,384]{1,0:T(8,128)(2,1)}, bf16[1024,384]{1,0:T(8,128)(2,1)}, u32[]{:S(2)}, u32[]{:S(2)}) %collective-permute-start.3) | collective-permute-done | bytes 786464 | tf_op jit(solution)/shard_map/ppermute | solution.py:15
  93.1 3.9 %copy.45 = bf16[1024,1024]{0,1:T(8,128)(2,1)} copy(bf16[1024,1024]{1,0:T(8,128)(2,1)} %param.6) | data formatting | bytes 4194304 | tf_op args[0]
  97.0 2.9 fusion.13
  100.0 4.8 %collective-permute-start.11 = (bf16[1024,384]{1,0:T(8,128)(2,1)}, bf16[1024,384]{1,0:T(8,128)(2,1)S(1)}, u32[]{:S(2)}, u32[]{:S(2)}) collective-permute-start(bf16[1024,384]{1,0:T(8,128)(2,1)} %collective-permute-done.10), channel_id=1, source_target_pairs={{0,120},{8,0},{16,8},{24,16},{32,24},{40,32},{48,40},{56,48},{64,5... | collective-permute-start | bytes 2359304 | tf_op jit(solution)/shard_map/ppermute | solution.py:17
  104.8 5.7 %collective-permute-done.4 = bf16[1024,384]{1,0:T(8,128)(2,1)} collective-permute-done((bf16[1024,384]{1,0:T(8,128)(2,1)}, bf16[1024,384]{1,0:T(8,128)(2,1)}, u32[]{:S(2)}, u32[]{:S(2)}) %collective-permute-start.4) | collective-permute-done | bytes 786464 | tf_op jit(solution)/shard_map/ppermute | solution.py:15
  110.7 2.5 fusion.33
  113.2 10.0 %collective-permute-done.11 = bf16[1024,384]{1,0:T(8,128)(2,1)S(1)} collective-permute-done((bf16[1024,384]{1,0:T(8,128)(2,1)}, bf16[1024,384]{1,0:T(8,128)(2,1)S(1)}, u32[]{:S(2)}, u32[]{:S(2)}) %collective-permute-start.11) | collective-permute-done | bytes 786464 | tf_op jit(solution)/shard_map/ppermute | solution.py:17
  123.2 5.4 %collective-permute-start.12 = (bf16[1024,384]{1,0:T(8,128)(2,1)S(1)}, bf16[1024,384]{1,0:T(8,128)(2,1)}, u32[]{:S(2)}, u32[]{:S(2)}) collective-permute-start(bf16[1024,384]{1,0:T(8,128)(2,1)S(1)} %collective-permute-done.11), channel_id=1, source_target_pairs={{0,120},{8,0},{16,8},{24,16},{32,24},{40,32},{48,40},{56,48},{64,5... | collective-permute-start | bytes 2359304 | tf_op jit(solution)/shard_map/ppermute | solution.py:17
  128.6 2.9 collective-permute-done.5
  131.5 6.1 %fusion.32 = f32[8,512,512]{2,1,0:T(8,128)} fusion(bf16[512,8,128]{0,2,1:T(8,128)(2,1)S(1)} %bitcast.46, bf16[512,8,128]{0,2,1:T(8,128)(2,1)} %bitcast.40), kind=kOutput, calls=%fused_computation.74 | convolution fusion | flops 536870912 | bytes 10485760 | tf_op jit(solution)/shard_map/thd,shd->hts/dot_general | solution.py:43
  137.6 4.5 %fusion.6 = f32[8,512,128]{2,1,0:T(8,128)S(1)} fusion(bf16[512,8,128]{0,2,1:T(8,128)(2,1)S(1)} %bitcast.38, f32[8,512,512]{2,1,0:T(8,128)S(1)} %fusion.33, pred[512,512]{1,0:T(8,128)(4,1)S(1)} %iota_compare_fusion), kind=kOutput, calls=%fused_computation.5 | convolution fusion | flops 3223322624 | bytes 11796480 | tf_op jit(solution)/shard_map/hts,she->the/dot_general | solution.py:45
  142.2 4.8 %collective-permute-start.13 = (bf16[1024,384]{1,0:T(8,128)(2,1)}, bf16[1024,384]{1,0:T(8,128)(2,1)}, u32[]{:S(2)}, u32[]{:S(2)}) collective-permute-start(bf16[1024,384]{1,0:T(8,128)(2,1)} %collective-permute-done.12), channel_id=1, source_target_pairs={{0,120},{8,0},{16,8},{24,16},{32,24},{40,32},{48,40},{56,48},{64,5... | collective-permute-start | bytes 2359304 | tf_op jit(solution)/shard_map/ppermute | solution.py:17
  148.5 2.5 bitcast_add_fusion
  151.1 8.2 %fusion.22 = f32[512,8,128]{2,0,1:T(8,128)} fusion(bf16[512,8,128]{0,2,1:T(8,128)(2,1)S(1)} %bitcast.36, f32[8,512,512]{2,1,0:T(8,128)} %fusion.32, pred[512,512]{1,0:T(8,128)(4,1)S(1)} %iota_compare_fusion), kind=kOutput, calls=%fused_computation.30 | convolution fusion | flops 3223322624 | bytes 11796480 | tf_op jit(solution)/shard_map/hts,she->the/dot_general | solution.py:45
  159.3 19.9 %collective-permute-done.13 = bf16[1024,384]{1,0:T(8,128)(2,1)} collective-permute-done((bf16[1024,384]{1,0:T(8,128)(2,1)}, bf16[1024,384]{1,0:T(8,128)(2,1)}, u32[]{:S(2)}, u32[]{:S(2)}) %collective-permute-start.13) | collective-permute-done | bytes 786464 | tf_op jit(solution)/shard_map/ppermute | solution.py:17
  179.2 5.5 %collective-permute-start.14 = (bf16[1024,384]{1,0:T(8,128)(2,1)}, bf16[1024,384]{1,0:T(8,128)(2,1)S(1)}, u32[]{:S(2)}, u32[]{:S(2)}) collective-permute-start(bf16[1024,384]{1,0:T(8,128)(2,1)} %collective-permute-done.13), channel_id=1, source_target_pairs={{0,120},{8,0},{16,8},{24,16},{32,24},{40,32},{48,40},{56,48},{64,5... | collective-permute-start | bytes 2359304 | tf_op jit(solution)/shard_map/ppermute | solution.py:17
  234.8 2.3 constant_dynamic-update-slice_fusion.5
  245.7 3.2 fusion.5
  248.9 4.8 %multiply_reduce_fusion = (f32[1024,8]{0,1:T(8,128)S(1)}, f32[1024,8,128]{2,0,1:T(8,128)S(1)}) fusion(f32[8,128,128]{2,1,0:T(8,128)S(1)} %fusion.5, bf16[1024,8,128]{0,2,1:T(8,128)(2,1)S(1)} %bitcast.34, f32[512,8,128]{2,0,1:T(8,128)} %bitcast_add_fusion, f32[512,8,128]{2,0,1:T(8,128)} %fusion.22), kind=kOutput, calls=%fused_computation.23 | convolution fusion | flops 1614798848 | bytes 11042816 | tf_op jit(solution)/shard_map/thd,hde->the/dot_general | solution.py:63
  255.2 2.7 copy.63
  257.9 21.9 %fusion.2 = bf16[1024,6144]{1,0:T(8,128)(2,1)} fusion(bf16[1024,1024]{0,1:T(8,128)(2,1)} %bitcast.47, bf16[1024,12288]{1,0:T(8,128)(2,1)} %constant_dynamic-update-slice_fusion, s32[]{:T(128)S(6)} %select_n.28), kind=kOutput, calls=%fused_computation.2 | convolution fusion | flops 12891193344 | bytes 27262980 | tf_op jit(solution)/shard_map/dot_general | solution.py:71
  279.8 71.1 %reduce-scatter.2.cloned.1.call-done = bf16[128,6144]{1,0:T(8,128)(2,1)} async-done(((bf16[1024,6144]{1,0:T(8,128)(2,1)}), bf16[128,6144]{1,0:T(8,128)(2,1)}) %reduce-scatter.2.cloned.1.call-update) | async-done | bytes 1572880 | tf_op jit(solution)/shard_map/reduce_scatter | solution.py:70
  350.8 2.9 add_convert_fusion
  (95 shorter events, 68.0 us)
Async XLA Ops:
  6.5 239.2 %all-gather.3.cloned.1.call-start = ((), (), s32[]{:S(2)}) async-start(), calls=%async_computation.2 | async-start | bytes 4456448 | tf_op jit(solution)/shard_map/all_gather | solution.py:57
  6.5 24.3 %collective-permute-start = (bf16[1024,384]{1,0:T(8,128)(2,1)}, bf16[1024,384]{1,0:T(8,128)(2,1)S(1)}, u32[]{:S(2)}, u32[]{:S(2)}) collective-permute-start(bf16[1024,384]{1,0:T(8,128)(2,1)} %param.10), channel_id=1, source_target_pairs={{0,8},{8,16},{16,24},{24,32},{32,40},{40,48},{48,56},{56,64},{64,7... | collective-permute-start | bytes 2359304 | tf_op jit(solution)/shard_map/ppermute | solution.py:15
  30.8 21.1 %copy-start.7 = (bf16[1024,384]{1,0:T(8,128)(2,1)}, bf16[1024,384]{1,0:T(8,128)(2,1)S(1)}, u32[]{:S(2)}) copy-start(bf16[1024,384]{1,0:T(8,128)(2,1)S(1)} %collective-permute-done) | copy-start | bytes 2359300
  30.8 21.1 %collective-permute-start.1 = (bf16[1024,384]{1,0:T(8,128)(2,1)S(1)}, bf16[1024,384]{1,0:T(8,128)(2,1)S(1)}, u32[]{:S(2)}, u32[]{:S(2)}) collective-permute-start(bf16[1024,384]{1,0:T(8,128)(2,1)S(1)} %collective-permute-done), channel_id=1, source_target_pairs={{0,8},{8,16},{16,24},{24,32},{32,40},{40,48},{48,56},{56,64},{64,7... | collective-permute-start | bytes 2359304 | tf_op jit(solution)/shard_map/ppermute | solution.py:15
  30.8 26.9 %collective-permute-start.8 = (bf16[1024,384]{1,0:T(8,128)(2,1)}, bf16[1024,384]{1,0:T(8,128)(2,1)}, u32[]{:S(2)}, u32[]{:S(2)}) collective-permute-start(bf16[1024,384]{1,0:T(8,128)(2,1)} %param.10), channel_id=1, source_target_pairs={{0,120},{8,0},{16,8},{24,16},{32,24},{40,32},{48,40},{56,48},{64,5... | collective-permute-start | bytes 2359304 | tf_op jit(solution)/shard_map/ppermute | solution.py:17
  51.9 20.3 %copy-start.9 = (bf16[1024,384]{1,0:T(8,128)(2,1)}, bf16[1024,384]{1,0:T(8,128)(2,1)S(1)}, u32[]{:S(2)}) copy-start(bf16[1024,384]{1,0:T(8,128)(2,1)S(1)} %collective-permute-done.1) | copy-start | bytes 2359300
  51.9 20.3 %collective-permute-start.2 = (bf16[1024,384]{1,0:T(8,128)(2,1)S(1)}, bf16[1024,384]{1,0:T(8,128)(2,1)}, u32[]{:S(2)}, u32[]{:S(2)}) collective-permute-start(bf16[1024,384]{1,0:T(8,128)(2,1)S(1)} %collective-permute-done.1), channel_id=1, source_target_pairs={{0,8},{8,16},{16,24},{24,32},{32,40},{40,48},{48,56},{56,64},{64,7... | collective-permute-start | bytes 2359304 | tf_op jit(solution)/shard_map/ppermute | solution.py:15
  57.7 19.6 %collective-permute-start.9 = (bf16[1024,384]{1,0:T(8,128)(2,1)}, bf16[1024,384]{1,0:T(8,128)(2,1)}, u32[]{:S(2)}, u32[]{:S(2)}) collective-permute-start(bf16[1024,384]{1,0:T(8,128)(2,1)} %collective-permute-done.8), channel_id=1, source_target_pairs={{0,120},{8,0},{16,8},{24,16},{32,24},{40,32},{48,40},{56,48},{64,5... | collective-permute-start | bytes 2359304 | tf_op jit(solution)/shard_map/ppermute | solution.py:17
  72.2 19.6 %collective-permute-start.3 = (bf16[1024,384]{1,0:T(8,128)(2,1)}, bf16[1024,384]{1,0:T(8,128)(2,1)}, u32[]{:S(2)}, u32[]{:S(2)}) collective-permute-start(bf16[1024,384]{1,0:T(8,128)(2,1)} %collective-permute-done.2), channel_id=1, source_target_pairs={{0,8},{8,16},{16,24},{24,32},{32,40},{40,48},{48,56},{56,64},{64,7... | collective-permute-start | bytes 2359304 | tf_op jit(solution)/shard_map/ppermute | solution.py:15
  74.5 18.6 %copy-start = (bf16[512,1024]{0,1:T(8,128)(2,1)}, bf16[512,1024]{0,1:T(8,128)(2,1)S(1)}, u32[]{:S(2)}) copy-start(bf16[512,1024]{0,1:T(8,128)(2,1)S(1)} %copy.79) | copy-start | bytes 3145732
  76.8 16.3 %copy-start.2 = (bf16[512,1024]{0,1:T(8,128)(2,1)}, bf16[512,1024]{0,1:T(8,128)(2,1)S(1)}, u32[]{:S(2)}) copy-start(bf16[512,1024]{0,1:T(8,128)(2,1)S(1)} %get-tuple-element.9) | copy-start | bytes 3145732
  77.2 22.7 %collective-permute-start.10 = (bf16[1024,384]{1,0:T(8,128)(2,1)}, bf16[1024,384]{1,0:T(8,128)(2,1)}, u32[]{:S(2)}, u32[]{:S(2)}) collective-permute-start(bf16[1024,384]{1,0:T(8,128)(2,1)} %collective-permute-done.9), channel_id=1, source_target_pairs={{0,120},{8,0},{16,8},{24,16},{32,24},{40,32},{48,40},{56,48},{64,5... | collective-permute-start | bytes 2359304 | tf_op jit(solution)/shard_map/ppermute | solution.py:17
  91.8 18.7 %collective-permute-start.4 = (bf16[1024,384]{1,0:T(8,128)(2,1)}, bf16[1024,384]{1,0:T(8,128)(2,1)}, u32[]{:S(2)}, u32[]{:S(2)}) collective-permute-start(bf16[1024,384]{1,0:T(8,128)(2,1)} %collective-permute-done.3), channel_id=1, source_target_pairs={{0,8},{8,16},{16,24},{24,32},{32,40},{40,48},{48,56},{56,64},{64,7... | collective-permute-start | bytes 2359304 | tf_op jit(solution)/shard_map/ppermute | solution.py:15
  93.0 257.8 %reduce-scatter.2.cloned.1.call-start = ((), (), s32[]{:S(2)}) async-start(), calls=%async_computation.1 | async-start | bytes 14155776 | tf_op jit(solution)/shard_map/reduce_scatter | solution.py:70
  97.0 40.6 %copy-start.1 = (bf16[512,1024]{0,1:T(8,128)(2,1)S(1)}, bf16[512,1024]{0,1:T(8,128)(2,1)}, u32[]{:S(2)}) copy-start(bf16[512,1024]{0,1:T(8,128)(2,1)} %copy-done) | copy-start | bytes 3145732
  97.0 51.5 %copy-start.5 = (f32[8,128,128]{2,1,0:T(8,128)S(1)}, f32[8,128,128]{2,1,0:T(8,128)}, u32[]{:S(2)}) copy-start(f32[8,128,128]{2,1,0:T(8,128)} %copy-done.4) | copy-start | bytes 1572868
  100.0 23.2 %collective-permute-start.11 = (bf16[1024,384]{1,0:T(8,128)(2,1)}, bf16[1024,384]{1,0:T(8,128)(2,1)S(1)}, u32[]{:S(2)}, u32[]{:S(2)}) collective-permute-start(bf16[1024,384]{1,0:T(8,128)(2,1)} %collective-permute-done.10), channel_id=1, source_target_pairs={{0,120},{8,0},{16,8},{24,16},{32,24},{40,32},{48,40},{56,48},{64,5... | collective-permute-start | bytes 2359304 | tf_op jit(solution)/shard_map/ppermute | solution.py:17
  110.5 20.9 %collective-permute-start.5 = (bf16[1024,384]{1,0:T(8,128)(2,1)}, bf16[1024,384]{1,0:T(8,128)(2,1)S(1)}, u32[]{:S(2)}, u32[]{:S(2)}) collective-permute-start(bf16[1024,384]{1,0:T(8,128)(2,1)} %collective-permute-done.4), channel_id=1, source_target_pairs={{0,8},{8,16},{16,24},{24,32},{32,40},{40,48},{48,56},{56,64},{64,7... | collective-permute-start | bytes 2359304 | tf_op jit(solution)/shard_map/ppermute | solution.py:15
  123.2 27.8 %copy-start.11 = (bf16[1024,384]{1,0:T(8,128)(2,1)}, bf16[1024,384]{1,0:T(8,128)(2,1)S(1)}, u32[]{:S(2)}) copy-start(bf16[1024,384]{1,0:T(8,128)(2,1)S(1)} %collective-permute-done.11) | copy-start | bytes 2359300
  123.2 19.0 %collective-permute-start.12 = (bf16[1024,384]{1,0:T(8,128)(2,1)S(1)}, bf16[1024,384]{1,0:T(8,128)(2,1)}, u32[]{:S(2)}, u32[]{:S(2)}) collective-permute-start(bf16[1024,384]{1,0:T(8,128)(2,1)S(1)} %collective-permute-done.11), channel_id=1, source_target_pairs={{0,120},{8,0},{16,8},{24,16},{32,24},{40,32},{48,40},{56,48},{64,5... | collective-permute-start | bytes 2359304 | tf_op jit(solution)/shard_map/ppermute | solution.py:17
  131.5 19.5 %copy-start.13 = (bf16[1024,384]{1,0:T(8,128)(2,1)}, bf16[1024,384]{1,0:T(8,128)(2,1)S(1)}, u32[]{:S(2)}) copy-start(bf16[1024,384]{1,0:T(8,128)(2,1)S(1)} %collective-permute-done.5) | copy-start | bytes 2359300
  131.5 17.0 %collective-permute-start.6 = (bf16[1024,384]{1,0:T(8,128)(2,1)S(1)}, bf16[1024,384]{1,0:T(8,128)(2,1)}, u32[]{:S(2)}, u32[]{:S(2)}) collective-permute-start(bf16[1024,384]{1,0:T(8,128)(2,1)S(1)} %collective-permute-done.5), channel_id=1, source_target_pairs={{0,8},{8,16},{16,24},{24,32},{32,40},{40,48},{48,56},{56,64},{64,7... | collective-permute-start | bytes 2359304 | tf_op jit(solution)/shard_map/ppermute | solution.py:15
  142.2 37.0 %collective-permute-start.13 = (bf16[1024,384]{1,0:T(8,128)(2,1)}, bf16[1024,384]{1,0:T(8,128)(2,1)}, u32[]{:S(2)}, u32[]{:S(2)}) collective-permute-start(bf16[1024,384]{1,0:T(8,128)(2,1)} %collective-permute-done.12), channel_id=1, source_target_pairs={{0,120},{8,0},{16,8},{24,16},{32,24},{40,32},{48,40},{56,48},{64,5... | collective-permute-start | bytes 2359304 | tf_op jit(solution)/shard_map/ppermute | solution.py:17
  148.5 36.8 %collective-permute-start.7 = (bf16[1024,384]{1,0:T(8,128)(2,1)}, bf16[1024,384]{1,0:T(8,128)(2,1)}, u32[]{:S(2)}, u32[]{:S(2)}) collective-permute-start(bf16[1024,384]{1,0:T(8,128)(2,1)} %collective-permute-done.6), channel_id=1, source_target_pairs={{0,8},{8,16},{16,24},{24,32},{32,40},{40,48},{48,56},{56,64},{64,7... | collective-permute-start | bytes 2359304 | tf_op jit(solution)/shard_map/ppermute | solution.py:15
  151.0 60.3 %copy-start.12 = (bf16[1024,384]{1,0:T(8,128)(2,1)S(1)}, bf16[1024,384]{1,0:T(8,128)(2,1)}, u32[]{:S(2)}) copy-start(bf16[1024,384]{1,0:T(8,128)(2,1)} %copy-done.11) | copy-start | bytes 2359300
  151.0 71.0 %copy-start.14 = (bf16[1024,384]{1,0:T(8,128)(2,1)S(1)}, bf16[1024,384]{1,0:T(8,128)(2,1)}, u32[]{:S(2)}) copy-start(bf16[1024,384]{1,0:T(8,128)(2,1)} %copy-done.13) | copy-start | bytes 2359300
  151.0 78.5 %copy-start.10 = (bf16[1024,384]{1,0:T(8,128)(2,1)S(1)}, bf16[1024,384]{1,0:T(8,128)(2,1)}, u32[]{:S(2)}) copy-start(bf16[1024,384]{1,0:T(8,128)(2,1)} %copy-done.9) | copy-start | bytes 2359300
  151.0 79.5 %copy-start.8 = (bf16[1024,384]{1,0:T(8,128)(2,1)S(1)}, bf16[1024,384]{1,0:T(8,128)(2,1)}, u32[]{:S(2)}) copy-start(bf16[1024,384]{1,0:T(8,128)(2,1)} %copy-done.7) | copy-start | bytes 2359300
  151.0 80.5 %copy-start.6 = (bf16[1024,384]{1,0:T(8,128)(2,1)S(1)}, bf16[1024,384]{1,0:T(8,128)(2,1)}, u32[]{:S(2)}) copy-start(bf16[1024,384]{1,0:T(8,128)(2,1)} %param.10) | copy-start | bytes 2359300
  179.2 37.5 %collective-permute-start.14 = (bf16[1024,384]{1,0:T(8,128)(2,1)}, bf16[1024,384]{1,0:T(8,128)(2,1)S(1)}, u32[]{:S(2)}, u32[]{:S(2)}) collective-permute-start(bf16[1024,384]{1,0:T(8,128)(2,1)} %collective-permute-done.13), channel_id=1, source_target_pairs={{0,120},{8,0},{16,8},{24,16},{32,24},{40,32},{48,40},{56,48},{64,5... | collective-permute-start | bytes 2359304 | tf_op jit(solution)/shard_map/ppermute | solution.py:17
  207.0 46.8 %copy-start.16 = (f32[1024]{0:T(1024)S(1)}, f32[1024]{0:T(1024)}, u32[]{:S(2)}) copy-start(f32[1024]{0:T(1024)} %param.9) | copy-start | bytes 12292
  257.9 93.0 %copy-start.15 = (bf16[128,6144]{1,0:T(8,128)(2,1)S(1)}, bf16[128,6144]{1,0:T(8,128)(2,1)}, u32[]{:S(2)}) copy-start(bf16[128,6144]{1,0:T(8,128)(2,1)} %param.11) | copy-start | bytes 4718596
  (2 other events, 29.7 us)
Sparse Core Ops, SparseCore 0:
  93.2 92.1 all-gather.2
  279.9 70.9 reduce-scatter.1
